TPU v7x, 256 devices: a whole 4x4x8 slice. The times are simulated.
256 devices in a mesh: hid: 32 (over y, z), wid: 4 (over x), ad: 2 (over core).
Axes of the slice: x: 4, y: 4, z: 8, core: 2. Of those that a mesh axis runs over, the one named last changes fastest.
Arguments:
- activations: bfloat16 [1536, 2, 8192], P(None, None, ('wid', 'ad')), may hold values from -6 to 6
- row_adapter_index: int32 [1536, 2], replicated, may hold values from 0 to 127, as said below
- gate_up_weight: bfloat16 [8192, 2, 14848], P(('wid', 'ad'), None, 'hid'), may hold values from -0.0625 to 0.0625
- down_weight: bfloat16 [14848, 8192], P('hid', ('wid', 'ad')), may hold values from -0.046875 to 0.046875
- adapter_shrink_weight: bfloat16 [128, 2, 64, 8192], P(('hid', 'wid'), 'ad'), may hold values from -0.0625 to 0.0625
- adapter_expand_weight: bfloat16 [128, 2, 64, 14848], P(('hid', 'wid'), 'ad'), may hold values from -0.75 to 0.75
Outputs:
- layer_out: bfloat16 [1536, 2, 8192], P('hid', None, ('wid', 'ad'))
Inputs may be any that keep to these rules, and one draw needn't show every extreme that they name: `row_adapter_index`: call rows 48 * h to 48 * h + 47 of both batches together block h. In every block no adapter is named more than 2 times, and one and the same adapter is named exactly 2 times in every block.
All inputs are finite; a program needn't handle non-finite values.
Results may differ from a plain program's by a relative error of at most 0.0064.
Values may be sent and summed in bfloat16 or wider, within the bound.
No kernel may reach another device: no remote copies, remote signals or barrier semaphores. Data moves between devices by JAX's collectives and lax.ppermute only.
A program may use at most 128 MiB of HBM per device.

v0:
```python
import jax
import jax.numpy as jnp
from jax import lax
from jax.sharding import PartitionSpec as P


def slot_targets(block_ids, wid_count, wid_index, hid_count, group_capacity):
    row_count = block_ids.shape[1]
    matches = block_ids[:, :, None] == block_ids[:, None, :]
    earlier = jnp.arange(row_count)[None, :] < jnp.arange(row_count)[:, None]
    row_rank = jnp.sum(jnp.logical_and(matches, earlier[None]).astype(jnp.int32), axis=2)
    owner_hid = block_ids // wid_count
    is_mine = block_ids % wid_count == wid_index
    return jnp.where(is_mine, owner_hid * group_capacity + row_rank, hid_count * group_capacity)


def process_group(
    activations,
    row_adapter_index,
    gate_up_weight,
    down_weight,
    adapter_shrink_weight,
    adapter_expand_weight,
    group_capacity,
):
    hid_count = lax.axis_size("hid")
    wid_count = lax.axis_size("wid")
    hid_index = lax.axis_index("hid")
    wid_index = lax.axis_index("wid")
    proj_index = lax.axis_index("ad")
    total_rows, batch_count, local_width = activations.shape
    block_rows = total_rows // hid_count
    flat_width = block_rows * batch_count
    ff_local = down_weight.shape[0]
    own_rows = lax.dynamic_slice_in_dim(activations, hid_index * block_rows, block_rows, 0)
    full_rows = lax.all_gather(own_rows, ("wid", "ad"), axis=2, tiled=True)
    full_rows = full_rows.reshape(flat_width, -1)
    block_ids = row_adapter_index.reshape(hid_count, flat_width)
    targets = slot_targets(block_ids, wid_count, wid_index, hid_count, group_capacity)
    own_targets = lax.dynamic_index_in_dim(targets, hid_index, 0, keepdims=False)
    send_rows = jnp.zeros((hid_count * group_capacity, full_rows.shape[1]), full_rows.dtype)
    send_rows = (
        send_rows.at[own_targets].set(full_rows, mode="drop").reshape(hid_count, group_capacity, -1)
    )
    shrink_weight = adapter_shrink_weight[0, 0]
    expand_weight = adapter_expand_weight[0, 0]
    rank_values = jnp.einsum(
        "hcd,rd->hcr",
        lax.all_to_all(send_rows, "hid", split_axis=0, concat_axis=0, tiled=True),
        shrink_weight,
        preferred_element_type=jnp.float32,
    ).astype(jnp.bfloat16)
    deltas = jnp.einsum(
        "hcr,rf->hcf", rank_values, expand_weight, preferred_element_type=jnp.float32
    ).astype(jnp.bfloat16)
    deltas = deltas.reshape(hid_count, group_capacity, hid_count, ff_local)
    returned = lax.all_to_all(deltas, "hid", split_axis=2, concat_axis=2, tiled=True)
    row_slot = targets % group_capacity
    owner_slot = targets // group_capacity
    slot_total = hid_count * group_capacity * hid_count
    positions = (
        jnp.arange(hid_count, dtype=jnp.int32)[:, None] * group_capacity + row_slot
    ) * hid_count + owner_slot
    positions = jnp.where(targets < hid_count * group_capacity, positions, slot_total)
    flat_rows = (
        jnp.arange(hid_count, dtype=jnp.int32)[:, None] * flat_width
        + jnp.arange(flat_width, dtype=jnp.int32)[None, :]
    )
    slot_rows = jnp.full((slot_total,), total_rows * batch_count, jnp.int32)
    slot_rows = slot_rows.at[positions.reshape(-1)].set(flat_rows.reshape(-1), mode="drop")
    acts_flat = activations.reshape(total_rows * batch_count, local_width)
    weights = gate_up_weight.reshape(gate_up_weight.shape[0], -1)
    partial_value = jnp.dot(acts_flat, weights, preferred_element_type=jnp.float32).reshape(
        -1, 2, ff_local
    )
    partial_value = partial_value.at[slot_rows, proj_index].add(
        returned.reshape(-1, ff_local).astype(jnp.float32), mode="drop"
    )
    summed = lax.psum(partial_value, ("wid", "ad"))
    hidden = (jax.nn.silu(summed[:, 0]) * summed[:, 1]).astype(jnp.bfloat16)
    hidden_rows3 = hidden.reshape(total_rows, batch_count, ff_local)
    result = lax.psum_scatter(
        jnp.einsum("rbf,fd->rbd", hidden_rows3, down_weight, preferred_element_type=jnp.float32),
        "hid",
        scatter_dimension=0,
        tiled=True,
    )
    return result.astype(jnp.bfloat16)


def local(
    activations,
    row_adapter_index,
    gate_up_weight,
    down_weight,
    adapter_shrink_weight,
    adapter_expand_weight,
):
    hid_count = lax.axis_size("hid")
    wid_count = lax.axis_size("wid")
    block_rows = activations.shape[0] // hid_count
    batch_total = activations.shape[1]
    group_capacity = max(2, 2 * batch_total * block_rows // (hid_count * wid_count))
    return process_group(
        activations,
        row_adapter_index,
        gate_up_weight,
        down_weight,
        adapter_shrink_weight,
        adapter_expand_weight,
        group_capacity,
    )


def solution(mesh):
    in_specs = (
        P(None, None, ("wid", "ad")),
        P(),
        P(("wid", "ad"), None, "hid"),
        P("hid", ("wid", "ad")),
        P(("hid", "wid"), "ad", None, None),
        P(("hid", "wid"), "ad", None, None),
    )
    out_specs = P("hid", None, ("wid", "ad"))
    return jax.shard_map(local, mesh=mesh, in_specs=in_specs, out_specs=out_specs, check_vma=False)
```

profile of v0, /device:TPU:4, one launch (start us, length us, event | category | flops | bytes accessed | tf_op | source)
XLA Modules:
  0.0 711.8 jit_solution(1682355030441047729)
XLA Ops:
  6.5 1.9 constant_dynamic-slice_fusion.4
  8.4 1.0 copy.46
  9.4 0.3 eq.38
  9.8 1.2 convert_reduce_fusion
  11.1 28.2 %all-gather.2.cloned.1.call-done = bf16[48,2,8192]{2,1,0:T(2,128)(2,1)} async-done(((bf16[48,2,1024]{2,1,0:T(2,128)(2,1)}), bf16[48,2,8192]{2,1,0:T(2,128)(2,1)}) %all-gather.2.cloned.1.call-update) | async-done | bytes 1572880 | tf_op jit(solution)/shard_map/all_gather | solution.py:36
  39.3 3.7 reshape.318
  42.9 4.5 scatter_custom_fusion.1
  47.4 2.5 reshape.299
  49.9 39.0 %all_to_all.10 = bf16[32,2,8192]{2,1,0:T(2,128)(2,1)} all-to-all(bf16[32,2,8192]{2,1,0:T(2,128)(2,1)} %reshape.299), channel_id=1, replica_groups=mesh['hid'=32,'wid'=4,'ad'=2] {'hid'}, dimensions={0} | all-to-all | bytes 2097152 | tf_op jit(solution)/shard_map/all_to_all | solution.py:49
  88.9 5.1 convolution_convert_fusion
  94.0 6.6 reshape.300
  100.6 5.0 copy.49
  105.7 5.3 all-to-all-start.1
  111.2 0.5 reshape.297
  111.7 10.2 %reshape.328 = bf16[3072,1024,1]{1,0,2:T(8,128)(2,1)} reshape(bf16[1536,2,1024]{2,1,0:T(2,128)(2,1)} %param.6) | data formatting | bytes 12582912 | tf_op jit(solution)/shard_map/reshape | solution.py:71
  122.2 11.7 %fusion.5 = f32[3072,2,464]{0,2,1:T(8,128)} fusion(bf16[3072,1024,1]{1,0,2:T(8,128)(2,1)} %reshape.328, bf16[1024,2,464]{0,2,1:T(8,128)(2,1)S(1)} %copy-done), kind=kOutput, calls=%fused_computation.12 | convolution fusion | flops 5838471168 | bytes 19595264 | tf_op jit(solution)/shard_map/dot_general | solution.py:73
  134.0 18.8 %copy.45 = f32[3072,2,464]{2,1,0:T(2,128)} copy(f32[3072,2,464]{0,2,1:T(8,128)} %fusion.5) | data formatting | bytes 22806528 | tf_op jit(solution)/shard_map/dot_general | solution.py:73
  152.8 16.0 %reshape.302 = f32[6144,464]{1,0:T(8,128)} reshape(f32[3072,2,464]{2,1,0:T(2,128)} %copy.45) | data formatting | bytes 22806528
  169.0 11.8 %scatter_custom_fusion = s32[2048]{0:T(1024)S(1)} fusion(s32[3072]{0:T(1024)S(1)} %bitcast.37, s32[3072]{0:T(1024)S(1)} %reshape.310, s32[]{:T(128)} %constant.74.clone.1), kind=kCustom, calls=%fused_computation.45 | custom fusion | bytes 8196 | tf_op jit(solution)/shard_map/scatter | solution.py:70
  181.0 4.7 copy.50
  185.7 22.4 %scatter_custom_fusion.2 = f32[6144,464]{1,0:T(8,128)} fusion(f32[6144,464]{1,0:T(8,128)} %reshape.302, s32[2048]{0:T(1024)S(1)} %broadcast_select_fusion, bf16[2048,464]{1,0:T(8,128)(2,1)} %bitcast.34), kind=kCustom, calls=%fused_computation.7 | custom fusion | flops 1900544 | bytes 13500416
  208.1 15.5 %reshape.303 = f32[3072,2,464]{2,1,0:T(2,128)} reshape(f32[6144,464]{1,0:T(8,128)} %scatter_custom_fusion.2) | data formatting | bytes 22806528 | tf_op jit(solution)/shard_map/scatter-add | solution.py:76
  223.9 147.6 %all-reduce.3.cloned.1.call-done = f32[3072,2,464]{2,1,0:T(2,128)} async-done(((f32[3072,2,464]{2,1,0:T(2,128)}), f32[3072,2,464]{2,1,0:T(2,128)}) %all-reduce.3.cloned.1.call-update) | async-done | bytes 11403280 | tf_op jit(solution)/shard_map/psum | solution.py:79
  371.6 42.2 %slice_reduce_fusion.1 = (f32[3072,464]{1,0:T(8,128)}, f32[3072,464]{1,0:T(8,128)}) fusion(f32[3072,2,464]{2,1,0:T(2,128)} %all-reduce.3.cloned.1.call-done), kind=kLoop, calls=%fused_computation.5 | loop fusion | bytes 22806528 | tf_op jit(solution)/shard_map/slice | solution.py:80
  413.8 8.4 %squeeze.19 = f32[1536,2,464]{2,1,0:T(2,128)} reshape(f32[3072,464]{1,0:T(8,128)} %get-tuple-element.5) | data formatting | bytes 11403264 | tf_op jit(solution)/shard_map/squeeze | solution.py:80
  422.2 10.2 %copy.52 = f32[1536,2,464]{0,2,1:T(8,128)} copy(f32[1536,2,464]{2,1,0:T(2,128)} %squeeze.19) | data formatting | bytes 11403264 | tf_op jit(solution)/shard_map/squeeze | solution.py:80
  432.4 8.4 %squeeze.20 = f32[1536,2,464]{2,1,0:T(2,128)} reshape(f32[3072,464]{1,0:T(8,128)} %get-tuple-element.6) | data formatting | bytes 11403264 | tf_op jit(solution)/shard_map/squeeze | solution.py:80
  440.8 10.3 %copy.53 = f32[1536,2,464]{0,2,1:T(8,128)} copy(f32[1536,2,464]{2,1,0:T(2,128)} %squeeze.20) | data formatting | bytes 11403264 | tf_op jit(solution)/shard_map/squeeze | solution.py:80
  451.1 10.9 %fusion.2 = f32[1536,2,1024]{2,0,1:T(8,128)} fusion(f32[1536,2,464]{0,2,1:T(8,128)} %copy.53, f32[1536,2,464]{0,2,1:T(8,128)} %copy.52, bf16[464,1024]{1,0:T(8,128)(2,1)S(1)} %copy-done.4), kind=kOutput, calls=%fused_computation.9 | convolution fusion | flops 2927788032 | bytes 24936448 | tf_op jit(solution)/shard_map/rbf,fd->rbd/dot_general | solution.py:83
  462.1 241.3 %reduce-scatter.2.cloned.1.call-done = f32[48,2,1024]{2,0,1:T(8,128)} async-done(((f32[1536,2,1024]{2,0,1:T(8,128)}), f32[48,2,1024]{2,0,1:T(8,128)}) %reduce-scatter.2.cloned.1.call-update) | async-done | bytes 393232 | tf_op jit(solution)/shard_map/reduce_scatter | solution.py:82
  703.4 1.0 convert_element_type.28
  704.4 0.9 copy.54
  (33 shorter events, 1.4 us)
Async XLA Ops:
  6.5 115.7 %copy-start = (bf16[1024,2,464]{0,2,1:T(8,128)(2,1)S(1)}, bf16[1024,2,464]{0,2,1:T(8,128)(2,1)}, u32[]{:S(2)}) copy-start(bf16[1024,2,464]{0,2,1:T(8,128)(2,1)} %param.8) | copy-start | bytes 5701636
  6.5 32.7 %all-gather.2.cloned.1.call-start = ((), (), s32[]{:S(2)}) async-start(), calls=%async_computation.3 | async-start | bytes 1769472 | tf_op jit(solution)/shard_map/all_gather | solution.py:36
  105.7 75.3 %all-to-all-start.1 = ((bf16[32,2,32,464]{3,1,0,2:T(2,128)(2,1)}), bf16[32,2,32,464]{3,1,0,2:T(2,128)(2,1)}, u32[]{:S(2)}, u32[]{:S(2)}) async-start(bf16[32,2,32,464]{3,1,0,2:T(2,128)(2,1)} %copy.49), calls=%async_computation.1 | async-start | bytes 4194304 | tf_op jit(solution)/shard_map/all_to_all | solution.py:57
  110.9 260.6 %all-reduce.3.cloned.1.call-start = ((), (), s32[]{:S(2)}) async-start(), calls=%async_computation.4 | async-start | bytes 25165824 | tf_op jit(solution)/shard_map/psum | solution.py:79
  152.8 28.0 %copy-start.3 = (s32[2]{0:T(128)S(1)}, s32[2]{0:T(128)}, u32[]{:S(2)}) copy-start(s32[2]{0:T(128)} %constant.98) | copy-start | bytes 28
  152.8 28.1 %copy-start.2 = (s32[2]{0:T(128)S(1)}, s32[2]{0:T(128)}, u32[]{:S(2)}) copy-start(s32[2]{0:T(128)} %constant.101) | copy-start | bytes 28
  223.6 479.8 %reduce-scatter.2.cloned.1.call-start = ((), (), s32[]{:S(2)}) async-start(), calls=%async_computation.5 | async-start | bytes 12976128 | tf_op jit(solution)/shard_map/reduce_scatter | solution.py:82
  440.8 10.3 %copy-start.4 = (bf16[464,1024]{1,0:T(8,128)(2,1)S(1)}, bf16[464,1024]{1,0:T(8,128)(2,1)}, u32[]{:S(2)}) copy-start(bf16[464,1024]{1,0:T(8,128)(2,1)} %param.9) | copy-start | bytes 2850820
  462.0 243.3 %copy-start.1 = (bf16[1024,2,464]{0,2,1:T(8,128)(2,1)S(1)}, bf16[1024,2,464]{0,2,1:T(8,128)(2,1)}, u32[]{:S(2)}) copy-start(bf16[1024,2,464]{0,2,1:T(8,128)(2,1)} %param.8) | copy-start | bytes 5701636
Sparse Core Ops, SparseCore 0:
  9.2 30.0 all-gather.1
  223.8 147.7 all-reduce.2
  462.2 241.1 reduce-scatter.1
where the time goes:
time: 715 us; the launch traced here: 712 us
  waiting for transfers between devices  417 us (58%)
  local copies, waits for them, and re-layouts  184 us (26%)
  blocking collectives  39 us (5%)
  matrix products  27.8 us (4%)
  other arithmetic  25.2 us (4%)
  between operations  13.3 us (2%)
    reduce_scatter x1, waiting for transfers between devices, process_group(): lax.psum_scatter(jnp.einsum('rbf,fd->rbd', hidden_rows3, down_weight, pre...  241 us
    psum x1, waiting for transfers between devices, process_group(): summed = lax.psum(partial_value, ('wid', 'ad'))  148 us
    slice x1, local copies, waits for them, and re-layouts, process_group(): hidden = (jax.nn.silu(summed[:, 0]) * summed[:, 1]).astype(jnp.bfloat16)  42.2 us
    all_to_all x1, blocking collectives, process_group(): lax.all_to_all(send_rows, 'hid', split_axis=0, concat_axis=0, tiled=True)  39 us
    squeeze x4, local copies, waits for them, and re-layouts, process_group(): hidden = (jax.nn.silu(summed[:, 0]) * summed[:, 1]).astype(jnp.bfloat16)  37.3 us
    all_gather x1, waiting for transfers between devices, process_group(): full_rows = lax.all_gather(own_rows, ('wid', 'ad'), axis=2, tiled=True)  28.2 us
    unnamed x4, other arithmetic  22.6 us
    dot_general x1, local copies, waits for them, and re-layouts, process_group(): jnp.dot(acts_flat, weights, preferred_element_type=jnp.float32)  18.8 us
  transfers between devices with their start and end apart: 4, of which 3 were waited for; matrix products, arithmetic and copies ran while one was open for 10% of the time, Pallas kernels for 0%

commit v1 on v0

v1 whole, which is shorter than its diff:
```python
import jax
import jax.numpy as jnp
from jax import lax
from jax.sharding import Mesh, PartitionSpec as P

CHUNKS = 3
Y, Z = 4, 8
F32 = jnp.float32
BF16 = jnp.bfloat16


def local(activations, row_adapter_index, gate_up_weight, down_weight, shrink, expand):
    hid = lax.axis_index(("y", "z"))
    wid = lax.axis_index("wid")
    ad = lax.axis_index("ad")
    n_hid = Y * Z
    total_rows, batches, width = activations.shape
    rows = total_rows * batches
    block = rows // n_hid
    part = block // CHUNKS
    units = down_weight.shape[0]
    rank = shrink.shape[2]
    slots = 2 * n_hid

    by_owner = expand[0, 0].reshape(rank, n_hid, units).transpose(1, 0, 2)
    expand_all = lax.all_to_all(by_owner, ("y", "z"), split_axis=0, concat_axis=0, tiled=True)

    def to_chunks(flat):
        return flat.reshape((n_hid, CHUNKS, part) + flat.shape[1:]).swapaxes(0, 1)

    acts = activations.reshape(n_hid, CHUNKS, part // 2, 2, width)
    acts = acts.swapaxes(0, 1).reshape(rows, width)
    ids = row_adapter_index.reshape(n_hid, block)
    same = ids[:, :, None] == ids[:, None, :]
    earlier = jnp.arange(block)[None, :] < jnp.arange(block)[:, None]
    place = jnp.sum((same & earlier[None]).astype(jnp.int32), axis=2)
    slot = 2 * jnp.arange(n_hid, dtype=jnp.int32)[:, None] + place
    owner, cls = ids // 4, ids % 4
    send_code = jnp.where(owner == hid, cls * slots + slot, -1)
    recv_code = jnp.where(cls == wid, owner * slots + slot, -1)
    send_code = to_chunks(send_code.reshape(rows)).reshape(rows)
    recv_code = to_chunks(recv_code.reshape(rows)).reshape(CHUNKS, rows // CHUNKS)

    pick = (jnp.arange(4 * slots, dtype=jnp.int32)[:, None] == send_code[None, :]).astype(BF16)
    picked = jnp.dot(pick, acts, preferred_element_type=F32).astype(BF16)
    picked = picked.reshape(4, 1, slots, width)
    picked = jnp.broadcast_to(picked, (4, 2, slots, width)).reshape(8, slots, width)
    got = lax.all_to_all(picked, ("wid", "ad"), split_axis=0, concat_axis=0, tiled=True)
    inner = jnp.einsum(
        "xsf,jxf->sj", got, shrink[0, 0].reshape(rank, 8, width), preferred_element_type=F32
    ).astype(BF16)
    inner_all = lax.all_to_all(
        jnp.broadcast_to(inner[None], (n_hid, slots, rank)),
        ("y", "z"), split_axis=0, concat_axis=0, tiled=True,
    )
    terms = jnp.einsum(
        "hsj,hju->hsu", inner_all, expand_all, preferred_element_type=F32
    ).astype(BF16).reshape(n_hid * slots, units)

    weights = gate_up_weight.transpose(1, 0, 2)
    chunk_rows = rows // CHUNKS
    half = chunk_rows // 2
    quarter = half // 4
    is_mine = (jnp.arange(2) == ad)[:, None, None]
    swap = [(0, 1), (1, 0)]
    acts = acts.reshape(CHUNKS, chunk_rows, width)
    outs = []
    for c in range(CHUNKS):
        base = jnp.einsum("rd,pdu->pru", acts[c], weights, preferred_element_type=F32)
        place_rows = (recv_code[c][:, None] == jnp.arange(n_hid * slots, dtype=jnp.int32)[None, :]).astype(BF16)
        delta = jnp.dot(place_rows, terms, preferred_element_type=F32).astype(BF16)
        value = base + jnp.where(is_mine, delta.astype(F32)[None], 0.0)
        away = lax.dynamic_slice_in_dim(value, (1 - ad) * half, half, 1).astype(BF16)
        keep = lax.dynamic_slice_in_dim(value, ad * half, half, 1)
        pair = keep + lax.ppermute(away, "ad", swap).astype(F32)
        pair = pair.astype(BF16).reshape(2, 4, quarter, units).swapaxes(0, 1)
        parts = lax.all_to_all(pair, "wid", split_axis=0, concat_axis=0, tiled=True)
        summed = jnp.sum(parts.astype(F32), axis=0)
        hidden = (jax.nn.silu(summed[0]) * summed[1]).astype(BF16)
        hidden = lax.all_gather(hidden, ("ad", "wid"), axis=0, tiled=True)
        partial = jnp.dot(hidden, down_weight, preferred_element_type=F32).astype(BF16)
        partial = lax.psum_scatter(partial, "y", scatter_dimension=0, tiled=True)
        outs.append(lax.psum_scatter(partial, "z", scatter_dimension=0, tiled=True))
    out = jnp.concatenate(outs, axis=0)
    return out.reshape(total_rows // n_hid, batches, -1)


def solution(mesh):
    grid = Mesh(mesh.devices.reshape(Y, Z, 4, 2), ("y", "z", "wid", "ad"))
    hid = ("y", "z")
    in_specs = (
        P(None, None, ("wid", "ad")),
        P(),
        P(("wid", "ad"), None, hid),
        P(hid, ("wid", "ad")),
        P(("y", "z", "wid"), "ad", None, None),
        P(("y", "z", "wid"), "ad", None, None),
    )
    return jax.shard_map(local, mesh=grid, in_specs=in_specs, out_specs=P(hid, None, ("wid", "ad")), check_vma=False)
```

time: 715 us -> 466 us (0.65)
  waiting for transfers between devices: 417 us -> 219 us
  local copies, waits for them, and re-layouts: 184 us -> 58.9 us
  blocking collectives: 39 us -> 92.1 us
  starting transfers between devices: 5.74 us -> 38.5 us
  other arithmetic: 25.2 us -> 7.22 us
    psum x1 -> x0, waiting for transfers between devices: 148 us -> none  [process_group(): summed = lax.psum(partial_value, ('wid', 'ad'))]
    reduce_scatter x1 -> x6, waiting for transfers between devices: 241 us -> 146 us  [the longest x3 117 us: local(): outs.append(lax.psum_scatter(partial, 'z', scatter_dimension=0, tiled=True))]
    all_gather x0 -> x3, blocking collectives: none -> 75.2 us  [local(): hidden = lax.all_gather(hidden, ('ad', 'wid'), axis=0, tiled=True)]
    all_to_all x1 -> x5, waiting for transfers between devices: 0.01 us -> 65.1 us  [the longest x1 37 us: local(): lax.all_to_all(by_owner, ('y', 'z'), split_axis=0, concat_axis=0, tiled=T...]
    slice x1 -> x2, local copies, waits for them, and re-layouts: 42.2 us -> 7.84 us  [the longest x1 7.71 us: local(): acts[c]]
    all_to_all x1 -> x5, starting transfers between devices: 5.25 us -> 36.6 us  [the longest x2 11.9 us: local(): parts = lax.all_to_all(pair, 'wid', split_axis=0, concat_axis=0, tiled=True)]
    all_gather x1 -> x0, waiting for transfers between devices: 28.2 us -> none  [process_group(): full_rows = lax.all_gather(own_rows, ('wid', 'ad'), axis=2, tiled=True)]
    squeeze x4 -> x3, local copies, waits for them, and re-layouts: 37.3 us -> 12.4 us  [local(): acts[c]]
  transfers between devices with their start and end apart: 4 -> 14, of which waited for: 3 -> 12; matrix products, arithmetic and copies ran while one was open for 10% -> 11% of each run, Pallas kernels for 0% -> 0%
where the time goes in v1:
time: 466 us; the launch traced here: 465 us
  waiting for transfers between devices  219 us (47%)
  blocking collectives  92.1 us (20%)
  local copies, waits for them, and re-layouts  58.9 us (13%)
  starting transfers between devices  38.5 us (8%)
  matrix products  34.8 us (7%)
  between operations  13.8 us (3%)
  other arithmetic  7.22 us (2%)
    reduce_scatter x3, waiting for transfers between devices, local(): outs.append(lax.psum_scatter(partial, 'z', scatter_dimension=0, tiled=True))  117 us
    all_gather x3, blocking collectives, local(): hidden = lax.all_gather(hidden, ('ad', 'wid'), axis=0, tiled=True)  75.2 us
    all_to_all x1, waiting for transfers between devices, local(): lax.all_to_all(by_owner, ('y', 'z'), split_axis=0, concat_axis=0, tiled=T...  37 us
    reduce_scatter x3, waiting for transfers between devices, local(): partial = lax.psum_scatter(partial, 'y', scatter_dimension=0, tiled=True)  28.5 us
    all_to_all x1, blocking collectives, local(): parts = lax.all_to_all(pair, 'wid', split_axis=0, concat_axis=0, tiled=True)  16.9 us
    all_to_all x2, waiting for transfers between devices, local(): parts = lax.all_to_all(pair, 'wid', split_axis=0, concat_axis=0, tiled=True)  15.1 us
    squeeze x3, local copies, waits for them, and re-layouts, local(): acts[c]  12.4 us
    all_to_all x2, starting transfers between devices, local(): parts = lax.all_to_all(pair, 'wid', split_axis=0, concat_axis=0, tiled=True)  11.9 us
  transfers between devices with their start and end apart: 14, of which 12 were waited for; matrix products, arithmetic and copies ran while one was open for 11% of the time, Pallas kernels for 0%

profile of v1, /device:TPU:4, one launch (start us, length us, event | category | flops | bytes accessed | tf_op | source)
XLA Modules:
  0.0 464.6 jit_solution(17052631867190961436)
XLA Ops:
  10.0 6.8 %copy.57 = bf16[32,3,16,2,1024]{4,3,2,0,1:T(2,128)(2,1)} copy(bf16[32,3,16,2,1024]{4,3,2,1,0:T(2,128)(2,1)} %bitcast.107) | data formatting | bytes 12582912 | tf_op jit(solution)/shard_map/reshape | solution.py:31
  16.7 10.2 %reshape.89 = bf16[3072,1024]{1,0:T(8,128)(2,1)} reshape(bf16[3,32,16,2,1024]{4,3,2,1,0:T(2,128)(2,1)} %bitcast.104) | data formatting | bytes 12582912 | tf_op jit(solution)/shard_map/reshape | solution.py:32
  26.9 4.6 fusion.17
  32.7 6.3 %all-to-all-start = ((bf16[8,64,1024]{2,1,0:T(8,128)(2,1)}), bf16[8,64,1024]{2,1,0:T(8,128)(2,1)}, u32[]{:S(2)}, u32[]{:S(2)}) async-start(bf16[8,64,1024]{2,1,0:T(8,128)(2,1)} %bitcast.7), calls=%async_computation | async-start | bytes 2097152 | tf_op jit(solution)/shard_map/all_to_all | solution.py:48
  40.7 11.2 %all-to-all-done = bf16[8,64,1024]{2,1,0:T(8,128)(2,1)} async-done(((bf16[8,64,1024]{2,1,0:T(8,128)(2,1)}), bf16[8,64,1024]{2,1,0:T(8,128)(2,1)}, u32[]{:S(2)}, u32[]{:S(2)}) %all-to-all-start) | async-done | bytes 1048608 | tf_op jit(solution)/shard_map/all_to_all | solution.py:48
  51.9 2.9 fusion.18
  56.0 10.0 %all-to-all-start.1 = ((bf16[32,2,2048]{2,1,0:T(2,128)(2,1)}), bf16[32,2,2048]{2,1,0:T(2,128)(2,1)S(1)}, u32[]{:S(2)}, u32[]{:S(2)}) async-start(bf16[32,2,2048]{2,1,0:T(2,128)(2,1)} %reshape.120), calls=%async_computation.1 | async-start | bytes 524288 | tf_op jit(solution)/shard_map/all_to_all | solution.py:52
  66.0 6.7 %reshape_squeeze.7 = bf16[64,32,464]{2,1,0:T(8,128)(2,1)} reshape(bf16[1,1,64,14848]{3,2,1,0:T(8,128)(2,1)} %param.11) | data formatting | bytes 3801088 | tf_op jit(solution)/shard_map/reshape;squeeze | solution.py:25
  72.7 4.1 copy.58
  78.5 8.4 %all-to-all-start.2 = ((bf16[32,64,464]{2,1,0:T(8,128)(2,1)}), bf16[32,64,464]{2,1,0:T(8,128)(2,1)}, u32[]{:S(2)}, u32[]{:S(2)}) async-start(bf16[32,64,464]{2,1,0:T(8,128)(2,1)} %bitcast.106), calls=%async_computation.2 | async-start | bytes 4194304 | tf_op jit(solution)/shard_map/all_to_all | solution.py:26
  87.1 7.7 %fusion.30 = (bf16[1,32,16,2,1024]{4,3,2,1,0:T(2,128)(2,1)}, bf16[1,32,16,2,1024]{4,3,2,1,0:T(2,128)(2,1)}, bf16[1,32,16,2,1024]{4,3,2,1,0:T(2,128)(2,1)}) fusion(bf16[3,32,16,2,1024]{4,3,2,1,0:T(2,128)(2,1)} %bitcast.105), kind=kLoop, calls=%fused_computation.79 | loop fusion | bytes 12582912 | tf_op jit(solution)/shard_map/slice | solution.py:69
  94.8 4.1 reshape.96
  99.2 37.0 %all-to-all-done.2 = bf16[32,64,464]{2,1,0:T(8,128)(2,1)} async-done(((bf16[32,64,464]{2,1,0:T(8,128)(2,1)}), bf16[32,64,464]{2,1,0:T(8,128)(2,1)}, u32[]{:S(2)}, u32[]{:S(2)}) %all-to-all-start.2) | async-done | bytes 1900576 | tf_op jit(solution)/shard_map/all_to_all | solution.py:26
  146.6 2.6 collective-permute-done
  149.2 3.0 bitcast_bitcast_fusion.2
  152.2 6.5 %all-to-all-start.3 = ((bf16[4,2,128,464]{2,3,1,0:T(8,128)(2,1)}), bf16[4,2,128,464]{2,3,1,0:T(8,128)(2,1)S(1)}, u32[]{:S(2)}, u32[]{:S(2)}) async-start(bf16[4,2,128,464]{2,3,1,0:T(8,128)(2,1)} %bitcast_bitcast_fusion.2), calls=%async_computation.3 | async-start | bytes 1900544 | tf_op jit(solution)/shard_map/all_to_all | solution.py:77
  158.8 4.1 reshape.99
  162.9 7.4 %all-to-all-done.3 = bf16[4,2,128,464]{2,3,1,0:T(8,128)(2,1)S(1)} async-done(((bf16[4,2,128,464]{2,3,1,0:T(8,128)(2,1)}), bf16[4,2,128,464]{2,3,1,0:T(8,128)(2,1)S(1)}, u32[]{:S(2)}, u32[]{:S(2)}) %all-to-all-start.3) | async-done | bytes 950304 | tf_op jit(solution)/shard_map/all_to_all | solution.py:77
  170.6 25.6 %all_gather.9 = bf16[1024,464]{0,1:T(8,128)(2,1)S(1)} all-gather(bf16[128,464]{0,1:T(8,128)(2,1)S(1)} %fusion.28), channel_id=1, replica_groups=mesh['y'=4,'z'=8,'wid'=4,'ad'=2] {'ad','wid'}, dimensions={0}, use_global_device_ids=true | all-gather | bytes 1069056 | tf_op jit(solution)/shard_map/all_gather | solution.py:80
  196.2 2.6 convolution_convert_fusion.2
  198.9 4.1 fusion.12
  209.1 5.5 %all-to-all-start.5 = ((bf16[4,2,128,464]{2,3,1,0:T(8,128)(2,1)}), bf16[4,2,128,464]{2,3,1,0:T(8,128)(2,1)S(1)}, u32[]{:S(2)}, u32[]{:S(2)}) async-start(bf16[4,2,128,464]{2,3,1,0:T(8,128)(2,1)} %bitcast_bitcast_fusion), calls=%async_computation.9 | async-start | bytes 1900544 | tf_op jit(solution)/shard_map/all_to_all | solution.py:77
  214.6 4.1 reshape.98
  218.8 7.7 %all-to-all-done.5 = bf16[4,2,128,464]{2,3,1,0:T(8,128)(2,1)S(1)} async-done(((bf16[4,2,128,464]{2,3,1,0:T(8,128)(2,1)}), bf16[4,2,128,464]{2,3,1,0:T(8,128)(2,1)S(1)}, u32[]{:S(2)}, u32[]{:S(2)}) %all-to-all-start.5) | async-done | bytes 950304 | tf_op jit(solution)/shard_map/all_to_all | solution.py:77
  226.7 25.1 %all_gather.11 = bf16[1024,464]{0,1:T(8,128)(2,1)S(1)} all-gather(bf16[128,464]{0,1:T(8,128)(2,1)S(1)} %fusion.24), channel_id=1, replica_groups=mesh['y'=4,'z'=8,'wid'=4,'ad'=2] {'ad','wid'}, dimensions={0}, use_global_device_ids=true | all-gather | bytes 1069056 | tf_op jit(solution)/shard_map/all_gather | solution.py:80
  254.8 4.1 fusion.14
  264.8 16.9 %all_to_all.30 = bf16[4,2,128,464]{2,3,1,0:T(8,128)(2,1)S(1)} all-to-all(bf16[4,2,128,464]{2,3,1,0:T(8,128)(2,1)S(1)} %bitcast_bitcast_fusion.1), channel_id=1, replica_groups=mesh['y'=4,'z'=8,'wid'=4,'ad'=2] {'wid'}, dimensions={0} | all-to-all | bytes 1900544 | tf_op jit(solution)/shard_map/all_to_all | solution.py:77
  281.9 24.5 %all_gather.10 = bf16[1024,464]{0,1:T(8,128)(2,1)S(1)} all-gather(bf16[128,464]{0,1:T(8,128)(2,1)S(1)} %fusion.26), channel_id=1, replica_groups=mesh['y'=4,'z'=8,'wid'=4,'ad'=2] {'ad','wid'}, dimensions={0}, use_global_device_ids=true | all-gather | bytes 1069056 | tf_op jit(solution)/shard_map/all_gather | solution.py:80
  310.2 28.5 %reduce-scatter.11.cloned.1.call-done = bf16[256,1024]{1,0:T(8,128)(2,1)} async-done(((bf16[1024,1024]{1,0:T(8,128)(2,1)}), bf16[256,1024]{1,0:T(8,128)(2,1)}) %reduce-scatter.11.cloned.1.call-update) | async-done | bytes 524304 | tf_op jit(solution)/shard_map/reduce_scatter | solution.py:82
  338.7 39.8 %reduce-scatter.9.cloned.1.call-done = bf16[32,1024]{1,0:T(8,128)(2,1)} async-done(((bf16[256,1024]{1,0:T(8,128)(2,1)}), bf16[32,1024]{1,0:T(8,128)(2,1)}) %reduce-scatter.9.cloned.1.call-update) | async-done | bytes 65552 | tf_op jit(solution)/shard_map/reduce_scatter | solution.py:83
  378.5 38.8 %reduce-scatter.17.cloned.1.call-done = bf16[32,1024]{1,0:T(8,128)(2,1)} async-done(((bf16[256,1024]{1,0:T(8,128)(2,1)}), bf16[32,1024]{1,0:T(8,128)(2,1)}) %reduce-scatter.17.cloned.1.call-update) | async-done | bytes 65552 | tf_op jit(solution)/shard_map/reduce_scatter | solution.py:83
  417.3 38.8 %reduce-scatter.13.cloned.1.call-done = bf16[32,1024]{1,0:T(8,128)(2,1)} async-done(((bf16[256,1024]{1,0:T(8,128)(2,1)}), bf16[32,1024]{1,0:T(8,128)(2,1)}) %reduce-scatter.13.cloned.1.call-update) | async-done | bytes 65552 | tf_op jit(solution)/shard_map/reduce_scatter | solution.py:83
  (80 shorter events, 41.0 us)
Async XLA Ops:
  6.5 135.7 %copy-start = (bf16[1024,2,464]{0,2,1:T(8,128)(2,1)S(1)}, bf16[1024,2,464]{0,2,1:T(8,128)(2,1)}, u32[]{:S(2)}) copy-start(bf16[1024,2,464]{0,2,1:T(8,128)(2,1)} %param.8) | copy-start | bytes 5701636
  31.5 7.5 %copy-start.6 = (bf16[1,1,64,8192]{3,2,1,0:T(8,128)(2,1)S(1)}, bf16[1,1,64,8192]{3,2,1,0:T(8,128)(2,1)}, u32[]{:S(2)}) copy-start(bf16[1,1,64,8192]{3,2,1,0:T(8,128)(2,1)} %param.10) | copy-start | bytes 3145732
  32.7 19.2 %all-to-all-start = ((bf16[8,64,1024]{2,1,0:T(8,128)(2,1)}), bf16[8,64,1024]{2,1,0:T(8,128)(2,1)}, u32[]{:S(2)}, u32[]{:S(2)}) async-start(bf16[8,64,1024]{2,1,0:T(8,128)(2,1)} %bitcast.7), calls=%async_computation | async-start | bytes 2097152 | tf_op jit(solution)/shard_map/all_to_all | solution.py:48
  56.0 22.4 %all-to-all-start.1 = ((bf16[32,2,2048]{2,1,0:T(2,128)(2,1)}), bf16[32,2,2048]{2,1,0:T(2,128)(2,1)S(1)}, u32[]{:S(2)}, u32[]{:S(2)}) async-start(bf16[32,2,2048]{2,1,0:T(2,128)(2,1)} %reshape.120), calls=%async_computation.1 | async-start | bytes 524288 | tf_op jit(solution)/shard_map/all_to_all | solution.py:52
  78.5 57.8 %all-to-all-start.2 = ((bf16[32,64,464]{2,1,0:T(8,128)(2,1)}), bf16[32,64,464]{2,1,0:T(8,128)(2,1)}, u32[]{:S(2)}, u32[]{:S(2)}) async-start(bf16[32,64,464]{2,1,0:T(8,128)(2,1)} %bitcast.106), calls=%async_computation.2 | async-start | bytes 4194304 | tf_op jit(solution)/shard_map/all_to_all | solution.py:26
  138.5 1.3 copy-start.2
  139.9 2.4 copy-start.5
  144.5 1.8 copy-start.1
  146.5 2.7 collective-permute-start
  152.2 18.1 %all-to-all-start.3 = ((bf16[4,2,128,464]{2,3,1,0:T(8,128)(2,1)}), bf16[4,2,128,464]{2,3,1,0:T(8,128)(2,1)S(1)}, u32[]{:S(2)}, u32[]{:S(2)}) async-start(bf16[4,2,128,464]{2,3,1,0:T(8,128)(2,1)} %bitcast_bitcast_fusion.2), calls=%async_computation.3 | async-start | bytes 1900544 | tf_op jit(solution)/shard_map/all_to_all | solution.py:77
  158.7 150.3 %reduce-scatter.7.cloned.1.call-start = ((), (), s32[]{:S(2)}) async-start(), calls=%async_computation.12 | async-start | bytes 2621440 | tf_op jit(solution)/shard_map/reduce_scatter | solution.py:82
  170.4 25.8 %copy-start.7 = (bf16[464,1024]{1,0:T(8,128)(2,1)S(1)}, bf16[464,1024]{1,0:T(8,128)(2,1)}, u32[]{:S(2)}) copy-start(bf16[464,1024]{1,0:T(8,128)(2,1)} %param.9) | copy-start | bytes 2850820
  198.9 4.2 copy-start.4
  205.4 2.6 collective-permute-start.2
  209.1 17.4 %all-to-all-start.5 = ((bf16[4,2,128,464]{2,3,1,0:T(8,128)(2,1)}), bf16[4,2,128,464]{2,3,1,0:T(8,128)(2,1)S(1)}, u32[]{:S(2)}, u32[]{:S(2)}) async-start(bf16[4,2,128,464]{2,3,1,0:T(8,128)(2,1)} %bitcast_bitcast_fusion), calls=%async_computation.9 | async-start | bytes 1900544 | tf_op jit(solution)/shard_map/all_to_all | solution.py:77
  214.6 95.0 %reduce-scatter.15.cloned.1.call-start = ((), (), s32[]{:S(2)}) async-start(), calls=%async_computation.16 | async-start | bytes 2621440 | tf_op jit(solution)/shard_map/reduce_scatter | solution.py:82
  226.5 25.3 %copy-start.8 = (bf16[464,1024]{1,0:T(8,128)(2,1)S(1)}, bf16[464,1024]{1,0:T(8,128)(2,1)}, u32[]{:S(2)}) copy-start(bf16[464,1024]{1,0:T(8,128)(2,1)} %param.9) | copy-start | bytes 2850820
  254.4 84.2 %reduce-scatter.11.cloned.1.call-start = ((), (), s32[]{:S(2)}) async-start(), calls=%async_computation.14 | async-start | bytes 2621440 | tf_op jit(solution)/shard_map/reduce_scatter | solution.py:82
  254.7 4.2 copy-start.3
  261.2 3.3 collective-permute-start.1
  264.8 41.5 %copy-start.9 = (bf16[464,1024]{1,0:T(8,128)(2,1)S(1)}, bf16[464,1024]{1,0:T(8,128)(2,1)}, u32[]{:S(2)}) copy-start(bf16[464,1024]{1,0:T(8,128)(2,1)} %param.9) | copy-start | bytes 2850820
  308.9 69.6 %reduce-scatter.9.cloned.1.call-start = ((), (), s32[]{:S(2)}) async-start(), calls=%async_computation.13 | async-start | bytes 589824 | tf_op jit(solution)/shard_map/reduce_scatter | solution.py:83
  309.5 107.8 %reduce-scatter.17.cloned.1.call-start = ((), (), s32[]{:S(2)}) async-start(), calls=%async_computation.17 | async-start | bytes 589824 | tf_op jit(solution)/shard_map/reduce_scatter | solution.py:83
  310.1 146.0 %reduce-scatter.13.cloned.1.call-start = ((), (), s32[]{:S(2)}) async-start(), calls=%async_computation.15 | async-start | bytes 589824 | tf_op jit(solution)/shard_map/reduce_scatter | solution.py:83
Sparse Core Ops, SparseCore 0:
  199.0 29.5 reduce-scatter.6
  254.6 30.2 reduce-scatter.14
  309.1 29.5 reduce-scatter.10
  341.0 37.4 reduce-scatter.8
  380.9 36.3 reduce-scatter.16
  419.7 36.3 reduce-scatter.12
